TPU v7x, 256 devices: a whole 4x4x8 slice. The times are simulated.
256 devices in a mesh: row: 4 (over x), col: 64 (over y, z, core).
Axes of the slice: x: 4, y: 4, z: 8, core: 2. Of those that a mesh axis runs over, the one named last changes fastest.
Arguments:
- activations: bfloat16 [8, 256, 8192], P('row')
- out_grads: bfloat16 [8, 256, 28672], P('row', None, 'col')
- valid_len: int32 [8], P('row'), may hold values from 1 to 256, 1024 in all
- weight: bfloat16 [8192, 28672], P('row', 'col'), may hold values from -0.0625 to 0.0625
- sketch: bfloat16 [28672, 512], P('col'), may hold values from -6 to 6
Outputs:
- basis: float32 [8192, 512], P(('row', 'col'))
- coeffs: float32 [512, 28672], P('row', 'col')
Inputs may be any that keep to these rules, and one draw needn't show every extreme that they name: `valid_len`: valid tokens of each sequence; at least one sequence fills all 256 slots.
All inputs are finite; a program needn't handle non-finite values. No bound on the sum of `valid_len` on one device may be relied on, other than what follows from the above.
Results may differ from a plain program's by a relative error of at most 0.01.
Values may be sent and summed in bfloat16 or wider, within the bound.
A program may use at most 64 MiB of HBM per device.

v0:
```python
import math
import jax
import jax.numpy as jnp
from jax import lax
from jax.sharding import PartitionSpec as P


def contract_rows(left, right):
    return lax.dot_general(
        left, right, (((0,), (0,)), ((), ())), preferred_element_type=jnp.float32
    )


def gram_local(sketch_rows):
    return lax.dot_general(
        sketch_rows, sketch_rows, (((0,), (0,)), ((), ())), precision=lax.Precision.HIGHEST
    )


def solve_basis(gram, sketch_rows):
    factor_low = jnp.linalg.cholesky(gram)
    return lax.linalg.triangular_solve(
        factor_low, sketch_rows, left_side=False, lower=True, transpose_a=True
    )


def orthonormal_shared(sketch_rows):
    gram = lax.psum(gram_local(sketch_rows), ("row", "col"))
    return solve_basis(gram, sketch_rows)


def reduce_sketch(left, right):
    return lax.psum_scatter(
        jnp.dot(left, right, preferred_element_type=jnp.float32),
        "col",
        scatter_dimension=0,
        tiled=True,
    )


def local(activations, out_grads, valid_len, weight, sketch):
    seq_dev, length, model_width = activations.shape
    rows_here, cols_here = weight.shape
    col_count = lax.axis_size("col")
    col_index = lax.axis_index("col")
    row_index = lax.axis_index("row")
    own_rows = rows_here // col_count
    own_start = col_index * own_rows
    positions = lax.iota(jnp.int32, length)
    raw_sketch = reduce_sketch(weight, sketch)
    partial_mass = jnp.zeros((model_width,), jnp.float32)
    for seq_index in range(seq_dev):
        valid = (positions < valid_len[seq_index]).astype(jnp.bfloat16)
        grad_block = contract_rows(activations[seq_index], out_grads[seq_index] * valid[:, None])
        partial_mass = partial_mass + jnp.sum(grad_block * grad_block, axis=1)
    fisher = lax.psum(partial_mass, ("row", "col"))
    total_mass = jnp.sum(fisher)
    own_mass = lax.dynamic_slice_in_dim(fisher, row_index * rows_here, rows_here, 0)
    row_scale = jnp.sqrt(own_mass / (total_mass / model_width + 1e-06))
    first_sketch = (
        lax.dynamic_slice_in_dim(row_scale, own_start, own_rows, 0)[:, None] * raw_sketch
    ).astype(jnp.bfloat16)
    scaled = (row_scale[:, None] * weight.astype(jnp.float32)).astype(jnp.bfloat16)
    proj_part = contract_rows(scaled, lax.all_gather(first_sketch, "col", axis=0, tiled=True))
    projected = lax.psum(proj_part, "row").astype(jnp.bfloat16)
    second_sketch = reduce_sketch(scaled, projected)
    second_basis = orthonormal_shared(second_sketch)
    group_second = lax.all_gather(second_basis.astype(jnp.bfloat16), "col", axis=0, tiled=True)
    coeff_raw = lax.psum_scatter(
        contract_rows(group_second, scaled).astype(jnp.bfloat16),
        "row",
        scatter_dimension=0,
        tiled=True,
    ).astype(jnp.float32)
    return (second_basis * math.sqrt(model_width), coeff_raw * math.sqrt(cols_here * col_count))


def solution(mesh):
    placed = (
        P("row", None, None),
        P("row", None, "col"),
        P("row"),
        P("row", "col"),
        P("col", None),
    )
    return jax.shard_map(
        local,
        mesh=mesh,
        in_specs=placed,
        out_specs=(P(("row", "col"), None), P("row", "col")),
        check_vma=False,
    )
```

profile of v0, /device:TPU:8, one launch (start us, length us, event | category | flops | bytes accessed | tf_op | source)
XLA Modules:
  0.0 952.2 jit_solution(8031663152801272860)
XLA Ops:
  8.2 4.7 fusion.51
  15.5 4.3 multiply_reduce_fusion
  19.8 4.4 multiply_reduce_fusion.1
  24.2 78.7 %psum.21 = f32[8192]{0:T(1024)S(1)} all-reduce(f32[8192]{0:T(1024)S(1)} %add.64), channel_id=1, replica_groups=mesh['row'=4,'col'=64] {'row','col'}, use_global_device_ids=true, to_apply=%region_2.0 | all-reduce | flops 8192 | bytes 65536 | tf_op jit(solution)/shard_map/psum | solution.py:56
  104.3 55.4 %reduce-scatter.6.cloned.1.call-done = f32[32,512]{1,0:T(8,128)} async-done(((f32[2048,512]{1,0:T(8,128)}), f32[32,512]{1,0:T(8,128)}) %reduce-scatter.6.cloned.1.call-update) | async-done | bytes 65552 | tf_op jit(solution)/shard_map/reduce_scatter | solution.py:33
  159.7 1.5 multiply_convert_fusion.6
  161.3 77.5 %all-gather.3.cloned.1.call-done = bf16[2048,512]{1,0:T(8,128)(2,1)} async-done(((bf16[32,512]{1,0:T(8,128)(2,1)}), bf16[2048,512]{1,0:T(8,128)(2,1)}) %all-gather.3.cloned.1.call-update) | async-done | bytes 2097168 | tf_op jit(solution)/shard_map/all_gather | solution.py:64
  238.8 3.6 fusion.6
  242.5 27.8 %all-reduce.5 = bf16[448,512]{1,0:T(8,128)(2,1)S(1)} all-reduce(f32[448,512]{1,0:T(8,128)} %fusion.6), channel_id=1, replica_groups=mesh['row'=4,'col'=64] {'row'}, use_global_device_ids=true, to_apply=%region_5.0 | all-reduce | flops 229376 | bytes 1376256 | tf_op jit(solution)/shard_map/psum | solution.py:65
  270.2 3.2 fusion.5
  273.5 141.3 %reduce-scatter.8.cloned.1.call-done = f32[32,512]{1,0:T(8,128)} async-done(((f32[2048,512]{1,0:T(8,128)}), f32[32,512]{1,0:T(8,128)}) %reduce-scatter.8.cloned.1.call-update) | async-done | bytes 65552 | tf_op jit(solution)/shard_map/reduce_scatter | solution.py:33
  414.8 3.0 fusion.52
  418.8 259.1 %all-reduce.4.cloned.1.call-done = f32[512,512]{0,1:T(8,128)} async-done(((f32[512,512]{0,1:T(8,128)}), f32[512,512]{0,1:T(8,128)}) %all-reduce.4.cloned.1.call-update) | async-done | bytes 1048592 | tf_op jit(solution)/shard_map/psum | solution.py:28
  677.9 1.6 copy.10
  682.0 11.7 %cholesky.104 = f32[128,128]{1,0:T(8,128)S(1)} custom-call(f32[128,128]{1,0:T(8,128)S(1)} %cholesky.266), custom_call_target="Cholesky" | custom-call | tf_op jit(solution)/shard_map/jit(cholesky)/cholesky | solution.py:21
  693.8 9.8 %custom-call.30 = f32[1,128,128]{1,2,0:T(8,128)S(1)} custom-call(f32[1,128,128]{2,1,0:T(8,128)S(1)} %get-tuple-element.29), custom_call_target="InvertDiagBlocksLowerTriangular" | custom-call | tf_op jit(solution)/shard_map/jit(cholesky)/cholesky | solution.py:21
  706.8 13.2 %cholesky.217 = f32[128,128]{1,0:T(8,128)} custom-call(f32[128,128]{1,0:T(8,128)} %cholesky.270), custom_call_target="Cholesky" | custom-call | tf_op jit(solution)/shard_map/jit(cholesky)/cholesky | solution.py:21
  720.0 1.5 select_reduce_fusion.2
  721.5 11.4 %custom-call.31 = f32[1,128,128]{1,2,0:T(8,128)} custom-call(f32[1,128,128]{2,1,0:T(8,128)} %get-tuple-element.26), custom_call_target="InvertDiagBlocksLowerTriangular" | custom-call | tf_op jit(solution)/shard_map/jit(cholesky)/cholesky | solution.py:21
  735.9 13.2 %cholesky.238 = f32[128,128]{1,0:T(8,128)} custom-call(f32[128,128]{1,0:T(8,128)} %cholesky.275), custom_call_target="Cholesky" | custom-call | tf_op jit(solution)/shard_map/jit(cholesky)/cholesky | solution.py:21
  749.1 1.5 select_reduce_fusion.1
  751.3 11.3 %custom-call.32 = f32[1,128,128]{1,2,0:T(8,128)} custom-call(f32[1,128,128]{2,1,0:T(8,128)} %get-tuple-element.23), custom_call_target="InvertDiagBlocksLowerTriangular" | custom-call | tf_op jit(solution)/shard_map/jit(cholesky)/cholesky | solution.py:21
  764.9 11.7 %cholesky.255 = f32[128,128]{1,0:T(8,128)S(1)} custom-call(f32[128,128]{1,0:T(8,128)S(1)} %convolution_subtract_fusion.2), custom_call_target="Cholesky" | custom-call | tf_op jit(solution)/shard_map/jit(cholesky)/cholesky | solution.py:21
  782.4 14.0 %while.1 = (s32[]{:T(128)}, f32[512,512]{1,0:T(8,128)}, s32[4,2]{0,1:T(2,128)S(1)}, f32[4,128,128]{2,1,0:T(8,128)}, s32[]{:T(128)}) while((s32[]{:T(128)}, f32[512,512]{1,0:T(8,128)}, s32[4,2]{0,1:T(2,128)S(1)}, f32[4,128,128]{2,1,0:T(8,128)}, s32[]{:T(128)}) %tuple.32), condition=%wide.while_cond, body=%wide.while_body.sunk | while | flops 2 | bytes 132705 | solution.py:22
  783.0 2.9 bitcast_dynamic-update-slice_fusion.2
  786.5 2.9 bitcast_dynamic-update-slice_fusion.2
  790.0 2.9 bitcast_dynamic-update-slice_fusion.2
  793.5 2.8 bitcast_dynamic-update-slice_fusion.2
  796.3 40.1 %custom-call.33 = f32[4,128,128]{1,2,0:T(8,128)S(1)} custom-call(f32[4,128,128]{2,1,0:T(8,128)} %get-tuple-element.9), custom_call_target="InvertDiagBlocksLowerTriangular" | custom-call | tf_op jit(solution)/shard_map/triangular_solve | solution.py:22
  841.4 75.5 %all-gather.5.cloned.1.call-done = bf16[2048,512]{1,0:T(8,128)(2,1)} async-done(((bf16[32,512]{1,0:T(8,128)(2,1)}), bf16[2048,512]{1,0:T(8,128)(2,1)}) %all-gather.5.cloned.1.call-update) | async-done | bytes 2097168 | tf_op jit(solution)/shard_map/all_gather | solution.py:68
  916.8 2.7 fusion.7
  921.2 22.2 %reduce-scatter.10.cloned.1.call-done = bf16[128,448]{1,0:T(8,128)(2,1)} async-done(((bf16[512,448]{1,0:T(8,128)(2,1)}), bf16[128,448]{1,0:T(8,128)(2,1)}) %reduce-scatter.10.cloned.1.call-update) | async-done | bytes 114704
  (71 shorter events, 30.9 us)
Async XLA Ops:
  7.2 1.0 copy-start
  7.2 152.5 %reduce-scatter.6.cloned.1.call-start = ((), (), s32[]{:S(2)}) async-start(), calls=%async_computation.3 | async-start | bytes 4259840 | tf_op jit(solution)/shard_map/reduce_scatter | solution.py:33
  12.9 0.7 copy-start.4
  12.9 2.6 copy-start.5
  12.9 225.9 %all-gather.3.cloned.1.call-start = ((), (), s32[]{:S(2)}) async-start(), calls=%async_computation.4 | async-start | bytes 2129920 | tf_op jit(solution)/shard_map/all_gather | solution.py:64
  19.8 219.0 %copy-start.1 = (bf16[2048,448]{0,1:T(8,128)(2,1)S(1)}, bf16[2048,448]{0,1:T(8,128)(2,1)}, u32[]{:S(2)}) copy-start(bf16[2048,448]{0,1:T(8,128)(2,1)} %param.8) | copy-start | bytes 5505028
  161.3 253.6 %reduce-scatter.8.cloned.1.call-start = ((), (), s32[]{:S(2)}) async-start(), calls=%async_computation.5 | async-start | bytes 4259840 | tf_op jit(solution)/shard_map/reduce_scatter | solution.py:33
  273.5 404.4 %all-reduce.4.cloned.1.call-start = ((), (), s32[]{:S(2)}) async-start(), calls=%async_computation.6 | async-start | bytes 2097152 | tf_op jit(solution)/shard_map/psum | solution.py:28
  417.8 499.0 %all-gather.5.cloned.1.call-start = ((), (), s32[]{:S(2)}) async-start(), calls=%async_computation.7 | async-start | bytes 2129920 | tf_op jit(solution)/shard_map/all_gather | solution.py:68
  680.9 1.0 copy-start.2
  734.0 102.5 %copy-start.3 = (f32[32,512]{1,0:T(8,128)S(1)}, f32[32,512]{1,0:T(8,128)}, u32[]{:S(2)}) copy-start(f32[32,512]{1,0:T(8,128)} %reduce-scatter.8.cloned.1.call-done) | copy-start | bytes 196612
  841.3 102.1 %reduce-scatter.10.cloned.1.call-start = ((), (), s32[]{:S(2)}) async-start(), calls=%async_computation.8 | async-start | bytes 655360
Sparse Core Ops, SparseCore 0:
  13.1 146.6 reduce-scatter.5
  163.1 75.7 all-gather.2
  273.6 141.1 reduce-scatter.7
  420.1 257.7 all-reduce.3
  841.4 75.3 all-gather.4
  920.7 22.6 reduce-scatter.9
where the time goes:
time: 961 us; the launch traced here: 952 us
  waiting for transfers between devices  631 us (66%)
  other arithmetic  136 us (14%)
  blocking collectives  106 us (11%)
  matrix products  37.2 us (4%)
  local copies, waits for them, and re-layouts  22.7 us (2%)
  between operations  17.8 us (2%)
    psum x1, waiting for transfers between devices, orthonormal_shared(): gram = lax.psum(gram_local(sketch_rows), ('row', 'col'))  259 us
    reduce_scatter x2, waiting for transfers between devices, reduce_sketch(): lax.psum_scatter(jnp.dot(left, right, preferred_element_type=jnp.float32)...  197 us
    another operation x14, other arithmetic, solve_basis(): factor_low = jnp.linalg.cholesky(gram)  87.3 us
    psum x1, blocking collectives, local(): fisher = lax.psum(partial_mass, ('row', 'col'))  78.7 us
    all_gather x1, waiting for transfers between devices, local(): lax.all_gather(first_sketch, 'col', axis=0, tiled=True)  77.5 us
    all_gather x1, waiting for transfers between devices, local(): lax.all_gather(second_basis.astype(jnp.bfloat16), 'col', axis=0, tiled=True)  75.5 us
    another operation x3, other arithmetic, solve_basis(): lax.linalg.triangular_solve(factor_low, sketch_rows, left_side=False, low...  42 us
    psum x1, blocking collectives, local(): projected = lax.psum(proj_part, 'row').astype(jnp.bfloat16)  27.8 us
  transfers between devices with their start and end apart: 6, of which 6 were waited for; matrix products, arithmetic and copies ran while one was open for 1% of the time, Pallas kernels for 0%

commit v1 on v0

--- a/solution.py
+++ b/solution.py
@@ -25,7 +25,7 @@
 
 
 def orthonormal_shared(sketch_rows):
-    gram = lax.psum(gram_local(sketch_rows), ("row", "col"))
+    gram = lax.psum(lax.psum(gram_local(sketch_rows), "row"), "col")
     return solve_basis(gram, sketch_rows)
 
 

time: 961 us -> 941 us (0.979)
  waiting for transfers between devices: 631 us -> 611 us
    psum x1 -> x2, waiting for transfers between devices: 259 us -> 240 us  [orthonormal_shared(): gram = lax.psum(lax.psum(gram_local(sketch_rows), 'row'), 'col')]
    unnamed x7 -> x8, waiting for transfers between devices: 22.3 us -> 22.4 us
  transfers between devices with their start and end apart: 6 -> 7, of which waited for: 6 -> 7; matrix products, arithmetic and copies ran while one was open for 1% -> 1% of each run, Pallas kernels for 0% -> 0%
where the time goes in v1:
time: 941 us; the launch traced here: 932 us
  waiting for transfers between devices  611 us (65%)
  other arithmetic  136 us (14%)
  blocking collectives  106 us (11%)
  matrix products  37.2 us (4%)
  local copies, waits for them, and re-layouts  22.7 us (2%)
  between operations  17.8 us (2%)
    psum x2, waiting for transfers between devices, orthonormal_shared(): gram = lax.psum(lax.psum(gram_local(sketch_rows), 'row'), 'col')  240 us
    reduce_scatter x2, waiting for transfers between devices, reduce_sketch(): lax.psum_scatter(jnp.dot(left, right, preferred_element_type=jnp.float32)...  197 us
    another operation x14, other arithmetic, solve_basis(): factor_low = jnp.linalg.cholesky(gram)  87.3 us
    psum x1, blocking collectives, local(): fisher = lax.psum(partial_mass, ('row', 'col'))  78.7 us
    all_gather x1, waiting for transfers between devices, local(): lax.all_gather(first_sketch, 'col', axis=0, tiled=True)  77.5 us
    all_gather x1, waiting for transfers between devices, local(): lax.all_gather(second_basis.astype(jnp.bfloat16), 'col', axis=0, tiled=True)  73.8 us
    another operation x3, other arithmetic, solve_basis(): lax.linalg.triangular_solve(factor_low, sketch_rows, left_side=False, low...  42 us
    psum x1, blocking collectives, local(): projected = lax.psum(proj_part, 'row').astype(jnp.bfloat16)  27.8 us
  transfers between devices with their start and end apart: 7, of which 7 were waited for; matrix products, arithmetic and copies ran while one was open for 1% of the time, Pallas kernels for 0%

profile of v1, /device:TPU:8, one launch (start us, length us, event | category | flops | bytes accessed | tf_op | source)
XLA Modules:
  0.0 931.9 jit_solution(876508169969290248)
XLA Ops:
  8.2 4.7 fusion.51
  15.5 4.3 multiply_reduce_fusion
  19.8 4.4 multiply_reduce_fusion.1
  24.2 78.7 %psum.28 = f32[8192]{0:T(1024)S(1)} all-reduce(f32[8192]{0:T(1024)S(1)} %add.66), channel_id=1, replica_groups=mesh['row'=4,'col'=64] {'row','col'}, use_global_device_ids=true, to_apply=%region_2.0 | all-reduce | flops 8192 | bytes 65536 | tf_op jit(solution)/shard_map/psum | solution.py:56
  104.3 55.4 %reduce-scatter.6.cloned.1.call-done = f32[32,512]{1,0:T(8,128)} async-done(((f32[2048,512]{1,0:T(8,128)}), f32[32,512]{1,0:T(8,128)}) %reduce-scatter.6.cloned.1.call-update) | async-done | bytes 65552 | tf_op jit(solution)/shard_map/reduce_scatter | solution.py:33
  159.7 1.5 multiply_convert_fusion.6
  161.3 77.5 %all-gather.3.cloned.1.call-done = bf16[2048,512]{1,0:T(8,128)(2,1)} async-done(((bf16[32,512]{1,0:T(8,128)(2,1)}), bf16[2048,512]{1,0:T(8,128)(2,1)}) %all-gather.3.cloned.1.call-update) | async-done | bytes 2097168 | tf_op jit(solution)/shard_map/all_gather | solution.py:64
  238.8 3.6 fusion.6
  242.5 27.8 %all-reduce.8 = bf16[448,512]{1,0:T(8,128)(2,1)S(1)} all-reduce(f32[448,512]{1,0:T(8,128)} %fusion.6), channel_id=1, replica_groups=mesh['row'=4,'col'=64] {'row'}, use_global_device_ids=true, to_apply=%region_5.0 | all-reduce | flops 229376 | bytes 1376256 | tf_op jit(solution)/shard_map/psum | solution.py:65
  270.2 3.2 fusion.5
  273.5 141.3 %reduce-scatter.8.cloned.1.call-done = f32[32,512]{1,0:T(8,128)} async-done(((f32[2048,512]{1,0:T(8,128)}), f32[32,512]{1,0:T(8,128)}) %reduce-scatter.8.cloned.1.call-update) | async-done | bytes 65552 | tf_op jit(solution)/shard_map/reduce_scatter | solution.py:33
  414.8 3.0 fusion.52
  417.9 50.4 %all-reduce.5.cloned.1.call-done = f32[512,512]{0,1:T(8,128)} async-done(((f32[512,512]{0,1:T(8,128)}), f32[512,512]{0,1:T(8,128)}) %all-reduce.5.cloned.1.call-update) | async-done | bytes 1048592 | tf_op jit(solution)/shard_map/psum | solution.py:28
  469.3 190.0 %all-reduce.7.cloned.1.call-done = f32[512,512]{0,1:T(8,128)} async-done(((f32[512,512]{0,1:T(8,128)}), f32[512,512]{0,1:T(8,128)}) %all-reduce.7.cloned.1.call-update) | async-done | bytes 1048592 | tf_op jit(solution)/shard_map/psum | solution.py:28
  659.3 1.6 copy.10
  663.3 11.7 %cholesky.104 = f32[128,128]{1,0:T(8,128)S(1)} custom-call(f32[128,128]{1,0:T(8,128)S(1)} %cholesky.266), custom_call_target="Cholesky" | custom-call | tf_op jit(solution)/shard_map/jit(cholesky)/cholesky | solution.py:21
  675.2 9.8 %custom-call.30 = f32[1,128,128]{1,2,0:T(8,128)S(1)} custom-call(f32[1,128,128]{2,1,0:T(8,128)S(1)} %get-tuple-element.29), custom_call_target="InvertDiagBlocksLowerTriangular" | custom-call | tf_op jit(solution)/shard_map/jit(cholesky)/cholesky | solution.py:21
  688.1 13.2 %cholesky.217 = f32[128,128]{1,0:T(8,128)} custom-call(f32[128,128]{1,0:T(8,128)} %cholesky.270), custom_call_target="Cholesky" | custom-call | tf_op jit(solution)/shard_map/jit(cholesky)/cholesky | solution.py:21
  701.3 1.5 select_reduce_fusion.2
  702.8 11.4 %custom-call.31 = f32[1,128,128]{1,2,0:T(8,128)} custom-call(f32[1,128,128]{2,1,0:T(8,128)} %get-tuple-element.26), custom_call_target="InvertDiagBlocksLowerTriangular" | custom-call | tf_op jit(solution)/shard_map/jit(cholesky)/cholesky | solution.py:21
  717.3 13.2 %cholesky.238 = f32[128,128]{1,0:T(8,128)} custom-call(f32[128,128]{1,0:T(8,128)} %cholesky.275), custom_call_target="Cholesky" | custom-call | tf_op jit(solution)/shard_map/jit(cholesky)/cholesky | solution.py:21
  732.7 11.3 %custom-call.32 = f32[1,128,128]{1,2,0:T(8,128)} custom-call(f32[1,128,128]{2,1,0:T(8,128)} %get-tuple-element.23), custom_call_target="InvertDiagBlocksLowerTriangular" | custom-call | tf_op jit(solution)/shard_map/jit(cholesky)/cholesky | solution.py:21
  746.2 11.7 %cholesky.255 = f32[128,128]{1,0:T(8,128)S(1)} custom-call(f32[128,128]{1,0:T(8,128)S(1)} %convolution_subtract_fusion.2), custom_call_target="Cholesky" | custom-call | tf_op jit(solution)/shard_map/jit(cholesky)/cholesky | solution.py:21
  763.7 14.0 %while.1 = (s32[]{:T(128)}, f32[512,512]{1,0:T(8,128)}, s32[4,2]{0,1:T(2,128)S(1)}, f32[4,128,128]{2,1,0:T(8,128)}, s32[]{:T(128)}) while((s32[]{:T(128)}, f32[512,512]{1,0:T(8,128)}, s32[4,2]{0,1:T(2,128)S(1)}, f32[4,128,128]{2,1,0:T(8,128)}, s32[]{:T(128)}) %tuple.32), condition=%wide.while_cond, body=%wide.while_body.sunk | while | flops 2 | bytes 132705 | solution.py:22
  764.3 2.9 bitcast_dynamic-update-slice_fusion.2
  767.8 2.9 bitcast_dynamic-update-slice_fusion.2
  771.4 2.9 bitcast_dynamic-update-slice_fusion.2
  774.9 2.8 bitcast_dynamic-update-slice_fusion.2
  777.7 40.1 %custom-call.33 = f32[4,128,128]{1,2,0:T(8,128)S(1)} custom-call(f32[4,128,128]{2,1,0:T(8,128)} %get-tuple-element.9), custom_call_target="InvertDiagBlocksLowerTriangular" | custom-call | tf_op jit(solution)/shard_map/triangular_solve | solution.py:22
  822.7 73.8 %all-gather.5.cloned.1.call-done = bf16[2048,512]{1,0:T(8,128)(2,1)} async-done(((bf16[32,512]{1,0:T(8,128)(2,1)}), bf16[2048,512]{1,0:T(8,128)(2,1)}) %all-gather.5.cloned.1.call-update) | async-done | bytes 2097168 | tf_op jit(solution)/shard_map/all_gather | solution.py:68
  896.5 2.7 fusion.7
  900.8 22.3 %reduce-scatter.10.cloned.1.call-done = bf16[128,448]{1,0:T(8,128)(2,1)} async-done(((bf16[512,448]{1,0:T(8,128)(2,1)}), bf16[128,448]{1,0:T(8,128)(2,1)}) %reduce-scatter.10.cloned.1.call-update) | async-done | bytes 114704
  (74 shorter events, 32.5 us)
Async XLA Ops:
  7.2 1.0 copy-start
  7.2 152.5 %reduce-scatter.6.cloned.1.call-start = ((), (), s32[]{:S(2)}) async-start(), calls=%async_computation.3 | async-start | bytes 4259840 | tf_op jit(solution)/shard_map/reduce_scatter | solution.py:33
  12.9 0.7 copy-start.4
  12.9 2.6 copy-start.5
  12.9 225.9 %all-gather.3.cloned.1.call-start = ((), (), s32[]{:S(2)}) async-start(), calls=%async_computation.4 | async-start | bytes 2129920 | tf_op jit(solution)/shard_map/all_gather | solution.py:64
  19.8 219.0 %copy-start.1 = (bf16[2048,448]{0,1:T(8,128)(2,1)S(1)}, bf16[2048,448]{0,1:T(8,128)(2,1)}, u32[]{:S(2)}) copy-start(bf16[2048,448]{0,1:T(8,128)(2,1)} %param.8) | copy-start | bytes 5505028
  161.3 253.6 %reduce-scatter.8.cloned.1.call-start = ((), (), s32[]{:S(2)}) async-start(), calls=%async_computation.5 | async-start | bytes 4259840 | tf_op jit(solution)/shard_map/reduce_scatter | solution.py:33
  273.5 194.7 %all-reduce.5.cloned.1.call-start = ((), (), s32[]{:S(2)}) async-start(), calls=%async_computation.6 | async-start | bytes 2097152 | tf_op jit(solution)/shard_map/psum | solution.py:28
  417.8 241.5 %all-reduce.7.cloned.1.call-start = ((), (), s32[]{:S(2)}) async-start(), calls=%async_computation.7 | async-start | bytes 2097152 | tf_op jit(solution)/shard_map/psum | solution.py:28
  468.2 428.2 %all-gather.5.cloned.1.call-start = ((), (), s32[]{:S(2)}) async-start(), calls=%async_computation.8 | async-start | bytes 2129920 | tf_op jit(solution)/shard_map/all_gather | solution.py:68
  662.3 1.0 copy-start.2
  715.3 102.5 %copy-start.3 = (f32[32,512]{1,0:T(8,128)S(1)}, f32[32,512]{1,0:T(8,128)}, u32[]{:S(2)}) copy-start(f32[32,512]{1,0:T(8,128)} %reduce-scatter.8.cloned.1.call-done) | copy-start | bytes 196612
  822.7 100.4 %reduce-scatter.10.cloned.1.call-start = ((), (), s32[]{:S(2)}) async-start(), calls=%async_computation.9 | async-start | bytes 655360
Sparse Core Ops, SparseCore 0:
  13.1 146.6 reduce-scatter.5
  163.1 75.7 all-gather.2
  273.6 141.1 reduce-scatter.7
  417.9 50.2 all-reduce.4
  471.5 187.7 all-reduce.6
  822.8 73.6 all-gather.4
  900.3 22.7 reduce-scatter.9
